TPU v7x, 256 devices: a whole 4x4x8 slice. The times are simulated.
256 devices in a mesh: group: 8 (over x, core), dom: 32 (over y, z).
Axes of the slice: x: 4, y: 4, z: 8, core: 2. Of those that a mesh axis runs over, the one named last changes fastest.
Arguments:
- flow_state: float32 [5, 1048576], P(None, ('group', 'dom')), may hold values from -6 to 6
- right_side: float32 [5, 1048576], P(None, ('group', 'dom')), may hold values from -6 to 6
- coupling: float32 [1048576], P(('group', 'dom')), may hold values from 0.03 to 0.3
- pivot_inv: float32 [32, 25, 32768], P(None, None, ('group', 'dom'))
- lower_blocks: float32 [32, 25, 32768], P(None, None, ('group', 'dom'))
- upper_blocks: float32 [32, 25, 32768], P(None, None, ('group', 'dom')), may hold values from -0.15 to 0.15
- face_up: int32 [8, 32, 256], P('group', 'dom'), may hold values from 0 to 4095, as said below
- face_down: int32 [8, 32, 256], P('group', 'dom'), may hold values from 0 to 4095, as said below
- coef_up: float32 [8, 32, 256], P('group', 'dom'), may hold values from 0.1 to 0.5
- coef_down: float32 [8, 32, 256], P('group', 'dom'), may hold values from 0.1 to 0.5
- send_cell: int32 [32, 32768], P(None, ('group', 'dom')), may hold values from 0 to 4095, as said below
- line_src: int32 [32, 32768], P(None, ('group', 'dom')), may hold values from 0 to 8191, as said below
- ret_slot: int32 [32, 32768], P(None, ('group', 'dom')), may hold values from 0 to 4095, as said below
- cell_src: int32 [1048576], P(('group', 'dom')), may hold values from 0 to 8191, as said below
Outputs:
- solution: float32 [5, 1048576], P(None, ('group', 'dom'))
- drive_next: float32 [5, 1048576], P(None, ('group', 'dom'))
Inputs may be any that keep to these rules, and one draw needn't show every extreme that they name: Within a group, the cells named by send_cell for all owners together with the own cells named by line_src cover every cell exactly once; for each sender and owner, the first entries, as many as the cells that sender sends that owner (at most 128), are used and the rest are unused; at most 128 cells go from one partition to one other owner, and this is reached for many pairs in every draw; a partition sends none of its cells to itself through send_cell. `ret_slot`: used entries point at the slot that holds the sent cell. `cell_src`: each cell's value returns to it from the slot that took it. `face_up`: distinct cells within one partition's list. `face_down`: distinct cells within one partition's list.
All inputs are finite; a program needn't handle non-finite values.
Results may differ from a plain program's by a relative error of at most 0.0001.
Values sent between devices are 32-bit elements; how exact they have to be, the bound alone decides.
A program may use at most 192 MiB of HBM per device.

v0:
```python
import jax
import jax.numpy as jnp
from jax import lax
from jax.sharding import PartitionSpec as P

SWEEPS = 2


def shifted(block, axis, distance):
    devices = range(lax.axis_size(axis))
    route = [(i - distance, i) for i in devices if i - distance in devices]
    return lax.ppermute(block, axis, route)


def apply_block(matrix, vector):
    nvar = vector.shape[0]
    return jnp.sum(matrix.reshape(nvar, nvar, -1) * vector[None, :, :], axis=1)


def solve_lines(line_vals, pivot_inv, lower_blocks, upper_blocks):
    nvar = line_vals.shape[0]
    line_len, _, line_count = pivot_inv.shape
    blocks = line_vals.reshape(nvar, line_len, line_count)
    forward_vals = []
    previous = None
    for cell_position in range(line_len):
        reduced = blocks[:, cell_position]
        if cell_position > 0:
            reduced = reduced - apply_block(lower_blocks[cell_position], previous)
        previous = apply_block(pivot_inv[cell_position], reduced)
        forward_vals.append(previous)
    results = [None] * line_len
    later = forward_vals[-1]
    results[-1] = later
    for cell_position in range(line_len - 2, -1, -1):
        later = forward_vals[cell_position] - apply_block(upper_blocks[cell_position], later)
        results[cell_position] = later
    return jnp.stack(results, axis=1).reshape(nvar, line_len * line_count)


def shards(
    flow_state,
    right_side,
    coupling,
    pivot_inv,
    lower_blocks,
    upper_blocks,
    face_up,
    face_down,
    coef_up,
    coef_down,
    send_cell,
    line_src,
    ret_slot,
    cell_src,
):
    nvar = flow_state.shape[0]
    cell_count = flow_state.shape[1]
    domains = lax.axis_size("dom")
    capacity = send_cell.shape[1]
    pool_base = domains * capacity
    up_cells = face_up.reshape(-1)
    down_cells = face_down.reshape(-1)
    up_coef = coef_up.reshape(-1)
    down_coef = coef_down.reshape(-1)
    slot_map = line_src.reshape(-1)

    def drive_term(values):
        zeros_col = jnp.zeros((nvar, 1), jnp.float32)
        beside = jnp.concatenate([zeros_col, values[:, :-1]], 1) + jnp.concatenate(
            [values[:, 1:], zeros_col], 1
        )
        total = right_side + coupling[None, :] * beside
        up_vals = values[:, up_cells]
        down_vals = values[:, down_cells]
        from_below = shifted(up_vals, "group", 1)
        from_above = shifted(down_vals, "group", -1)
        total = total.at[:, down_cells].add(down_coef[None, :] * from_below)
        total = total.at[:, up_cells].add(up_coef[None, :] * from_above)
        return total

    peer_maps = lax.all_to_all(send_cell, "dom", split_axis=0, concat_axis=0, tiled=True)
    remote = slot_map < pool_base
    clipped = jnp.minimum(slot_map, pool_base - 1)
    global_idx = clipped // capacity * cell_count + peer_maps.reshape(-1)[clipped]
    own_idx = jnp.clip(slot_map - pool_base, 0, cell_count - 1)
    state_now = flow_state
    for sweep_idx in range(SWEEPS):
        drive_vals = drive_term(state_now)
        whole = lax.all_gather(drive_vals, "dom", axis=1, tiled=True)
        line_vals = jnp.where(remote[None, :], whole[:, global_idx], drive_vals[:, own_idx])
        solved = solve_lines(line_vals, pivot_inv, lower_blocks, upper_blocks)
        outgoing = solved[:, ret_slot]
        returned = lax.all_to_all(outgoing, "dom", split_axis=1, concat_axis=1, tiled=True)
        pooled = jnp.concatenate([returned.reshape(nvar, pool_base), solved], 1)
        state_now = pooled[:, cell_src]
    drive_last = drive_term(state_now)
    return (state_now, drive_last)


def solution(mesh):
    return jax.shard_map(
        shards,
        mesh=mesh,
        in_specs=(
            P(None, ("group", "dom")),
            P(None, ("group", "dom")),
            P(("group", "dom")),
            P(None, None, ("group", "dom")),
            P(None, None, ("group", "dom")),
            P(None, None, ("group", "dom")),
            P("group", "dom", None),
            P("group", "dom", None),
            P("group", "dom", None),
            P("group", "dom", None),
            P(None, ("group", "dom")),
            P(None, ("group", "dom")),
            P(None, ("group", "dom")),
            P(("group", "dom")),
        ),
        out_specs=(P(None, ("group", "dom")), P(None, ("group", "dom"))),
        check_vma=False,
    )
```

profile of v0, /device:TPU:1, one launch (start us, length us, event | category | flops | bytes accessed | tf_op | source)
XLA Modules:
  0.0 1229.4 jit_solution(4603384156076529335)
XLA Ops:
  8.7 1.5 copy.514
  11.0 4.5 collective-permute-start
  16.2 1.9 collective-permute-start.1
  19.1 2.8 scatter_custom_fusion
  22.5 2.8 scatter_custom_fusion.1
  26.7 11.2 all-to-all-start
  40.2 3.4 slice_reduce_fusion.2
  47.5 1.3 fusion.25
  48.9 2.0 slice_reduce_fusion.5
  50.9 1.3 reshape_squeeze.376
  52.2 1.3 reshape_squeeze.379
  53.5 1.3 reshape_squeeze.378
  54.8 1.3 reshape_squeeze.382
  56.2 1.3 reshape_squeeze.381
  57.5 1.3 reshape_squeeze.385
  58.8 1.3 reshape_squeeze.384
  60.1 1.3 reshape_squeeze.388
  61.4 1.3 reshape_squeeze.387
  63.4 1.3 reshape_squeeze.390
  65.3 1.3 reshape_squeeze.393
  67.2 1.3 reshape_squeeze.396
  69.2 1.3 reshape_squeeze.399
  74.1 1.3 reshape_squeeze.412
  75.4 1.3 reshape_squeeze.411
  76.7 1.3 reshape_squeeze.415
  78.0 1.3 reshape_squeeze.414
  79.4 1.3 reshape_squeeze.418
  80.7 1.3 reshape_squeeze.417
  83.3 1.3 reshape_squeeze.420
  84.6 1.3 reshape_squeeze.424
  85.9 1.3 reshape_squeeze.423
  87.9 1.3 reshape_squeeze.426
  89.8 1.3 reshape_squeeze.429
  95.0 14.1 %gather_fusion.4 = f32[4096,5]{1,0:T(8,128)} fusion(f32[5,4096]{0,1:T(8,128)S(1)} %copy-done.1, s32[4096]{0:T(1024)S(1)} %broadcast_clamp_fusion.1), kind=kCustom, calls=%fused_computation.4 | custom fusion | bytes 180224 | tf_op jit(solution)/shard_map/gather | solution.py:91
  109.0 2.2 copy.518
  111.2 23.2 %gather_fusion.2 = s32[4096]{0:T(1024)S(1)} fusion(s32[4096]{0:T(1024)S(1)} %bitcast.448, s32[4096]{0:T(1024)} %broadcast_clamp_fusion.2), kind=kCustom, calls=%fused_computation.2 | custom fusion | bytes 49152 | tf_op jit(solution)/shard_map/gather | solution.py:85
  134.5 325.0 %all-gather.3.cloned.1.call-done = f32[5,131072]{0,1:T(8,128)} async-done(((f32[5,4096]{0,1:T(8,128)}), f32[5,131072]{0,1:T(8,128)}) %all-gather.3.cloned.1.call-update) | async-done | bytes 2621456 | tf_op jit(solution)/shard_map/all_gather | solution.py:90
  459.5 62.3 %gather_fusion.3 = f32[4096,5]{1,0:T(8,128)S(1)} fusion(f32[5,131072]{0,1:T(8,128)} %all-gather.3.cloned.1.call-done, s32[4096]{0:T(1024)S(1)} %broadcast_clamp_fusion), kind=kCustom, calls=%fused_computation.3 | custom fusion | bytes 180224 | tf_op jit(solution)/shard_map/gather | solution.py:91
  557.4 14.1 %gather_fusion.5 = f32[4096,5]{1,0:T(8,128)} fusion(f32[5,4096]{0,1:T(8,128)S(1)} %bitcast.451, s32[4096]{0:T(1024)S(1)} %copy-done.17), kind=kCustom, calls=%fused_computation.5 | custom fusion | bytes 180224 | tf_op jit(solution)/shard_map/gather | solution.py:93
  571.4 2.2 copy.520
  573.7 15.9 %all_to_all.19 = f32[5,32,128]{2,0,1:T(8,128)S(1)} all-to-all(f32[5,32,128]{2,0,1:T(8,128)S(1)} %bitcast.468), channel_id=1, replica_groups=mesh['group'=8,'dom'=32] {'dom'}, dimensions={1} | all-to-all | bytes 163840 | tf_op jit(solution)/shard_map/all_to_all | solution.py:94
  589.6 2.0 copy.521
  591.5 3.8 pad_maximum_fusion
  595.3 13.0 %gather_fusion.6 = f32[4096,5]{1,0:T(8,128)S(1)} fusion(f32[5,8192]{0,1:T(8,128)} %pad_maximum_fusion, s32[4096]{0:T(1024)S(1)} %copy-done.12), kind=kCustom, calls=%fused_computation.6 | custom fusion | bytes 180224 | tf_op jit(solution)/shard_map/gather | solution.py:96
  608.9 1.6 gather_fusion.7
  610.6 1.5 gather_fusion.8
  612.1 5.9 collective-permute-start.2
  618.1 2.1 collective-permute-start.3
  621.0 3.2 scatter_custom_fusion.2
  624.7 3.1 scatter_custom_fusion.3
  627.9 1.3 copy-done.2
  629.2 12.4 %gather_fusion.10 = f32[4096,5]{1,0:T(8,128)S(1)} fusion(f32[5,4096]{0,1:T(8,128)} %copy-done.2, s32[4096]{0:T(1024)S(1)} %copy-done.9), kind=kCustom, calls=%fused_computation.10 | custom fusion | bytes 180224 | tf_op jit(solution)/shard_map/gather | solution.py:91
  642.2 412.6 %all-gather.5.cloned.1.call-done = f32[5,131072]{0,1:T(8,128)} async-done(((f32[5,4096]{0,1:T(8,128)}), f32[5,131072]{0,1:T(8,128)}) %all-gather.5.cloned.1.call-update) | async-done | bytes 2621456 | tf_op jit(solution)/shard_map/all_gather | solution.py:90
  1054.8 62.3 %gather_fusion.9 = f32[4096,5]{1,0:T(8,128)S(1)} fusion(f32[5,131072]{0,1:T(8,128)} %all-gather.5.cloned.1.call-done, s32[4096]{0:T(1024)S(1)} %copy-done.11), kind=kCustom, calls=%fused_computation.9 | custom fusion | bytes 180224 | tf_op jit(solution)/shard_map/gather | solution.py:91
  1152.6 14.1 %gather_fusion.11 = f32[4096,5]{1,0:T(8,128)} fusion(f32[5,4096]{0,1:T(8,128)S(1)} %bitcast.449, s32[4096]{0:T(1024)S(1)} %copy-done.18), kind=kCustom, calls=%fused_computation.11 | custom fusion | bytes 180224 | tf_op jit(solution)/shard_map/gather | solution.py:93
  1166.7 2.2 copy.529
  1168.9 15.9 %all_to_all.20 = f32[5,32,128]{2,0,1:T(8,128)S(1)} all-to-all(f32[5,32,128]{2,0,1:T(8,128)S(1)} %bitcast.469), channel_id=1, replica_groups=mesh['group'=8,'dom'=32] {'dom'}, dimensions={1} | all-to-all | bytes 163840 | tf_op jit(solution)/shard_map/all_to_all | solution.py:94
  1184.8 2.0 copy.530
  1186.8 3.8 pad_maximum_fusion.1
  1190.6 13.0 %gather_fusion.12 = f32[4096,5]{1,0:T(8,128)S(1)} fusion(f32[5,8192]{0,1:T(8,128)} %pad_maximum_fusion.1, s32[4096]{0:T(1024)S(1)} %copy-done.13), kind=kCustom, calls=%fused_computation.12 | custom fusion | bytes 180224 | tf_op jit(solution)/shard_map/gather | solution.py:96
  1206.1 5.9 collective-permute-start.4
  1212.1 1.9 collective-permute-start.5
  1214.8 2.9 scatter_custom_fusion.4
  1218.4 2.9 scatter_custom_fusion.5
  (598 shorter events, 100.3 us)
Async XLA Ops:
  7.2 11.0 copy-start.3
  7.2 11.1 copy-start.5
  7.2 11.1 copy-start.14
  7.2 452.3 %all-gather.3.cloned.1.call-start = ((), (), s32[]{:S(2)}) async-start(), calls=%async_computation.3 | async-start | bytes 69206016 | tf_op jit(solution)/shard_map/all_gather | solution.py:90
  8.0 11.1 copy-start.51
  8.7 13.8 %copy-start.50 = (s32[256,1]{0,1:T(1,128)}, s32[256,1]{0,1:T(1,128)S(1)}, u32[]{:S(2)}) copy-start(s32[256,1]{0,1:T(1,128)S(1)} %compare_select_fusion.8) | copy-start | bytes 3076
  10.2 8.9 copy-start.44
  10.2 0.8 copy-start.43
  10.3 11.6 copy-start.42
  11.0 8.1 collective-permute-start
  16.2 6.3 collective-permute-start.1
  18.4 4.1 copy-start.47
  22.5 15.6 %copy-start.7 = (f32[32,25,128]{2,0,1:T(8,128)S(1)}, f32[32,25,128]{2,0,1:T(8,128)}, u32[]{:S(2)}) copy-start(f32[32,25,128]{2,0,1:T(8,128)} %param.18) | copy-start | bytes 1228804
  22.5 16.6 %copy-start.6 = (f32[32,25,128]{2,0,1:T(8,128)S(1)}, f32[32,25,128]{2,0,1:T(8,128)}, u32[]{:S(2)}) copy-start(f32[32,25,128]{2,0,1:T(8,128)} %param.17) | copy-start | bytes 1228804
  25.3 1.3 copy-start
  25.3 20.8 %copy-start.19 = (s32[32,128]{1,0:T(8,128)S(1)}, s32[32,128]{1,0:T(8,128)}, u32[]{:S(2)}) copy-start(s32[32,128]{1,0:T(8,128)} %param.25) | copy-start | bytes 49156
  26.7 84.6 %all-to-all-start = ((s32[32,1,128]{2,1,0:T(1,128)}), s32[32,1,128]{2,1,0:T(1,128)S(1)}, u32[]{:S(2)}, u32[]{:S(2)}) async-start(s32[32,1,128]{2,1,0:T(1,128)} %bitcast.11), calls=%async_computation | async-start | bytes 32768 | tf_op jit(solution)/shard_map/all_to_all | solution.py:82
  37.9 1016.9 %all-gather.5.cloned.1.call-start = ((), (), s32[]{:S(2)}) async-start(), calls=%async_computation.4 | async-start | bytes 69206016 | tf_op jit(solution)/shard_map/all_gather | solution.py:90
  44.8 42.5 %copy-start.36 = (f32[25,128]{1,0:T(8,128)S(1)}, f32[25,128]{1,0:T(8,128)}, u32[]{:S(2)}) copy-start(f32[25,128]{1,0:T(8,128)} %get-tuple-element.25) | copy-start | bytes 38404
  44.8 49.6 %copy-start.30 = (f32[25,128]{1,0:T(8,128)S(1)}, f32[25,128]{1,0:T(8,128)}, u32[]{:S(2)}) copy-start(f32[25,128]{1,0:T(8,128)} %get-tuple-element.69) | copy-start | bytes 38404
  44.8 49.6 %copy-start.34 = (f32[25,128]{1,0:T(8,128)S(1)}, f32[25,128]{1,0:T(8,128)}, u32[]{:S(2)}) copy-start(f32[25,128]{1,0:T(8,128)} %get-tuple-element.81) | copy-start | bytes 38404
  44.8 49.6 %copy-start.35 = (f32[25,128]{1,0:T(8,128)S(1)}, f32[25,128]{1,0:T(8,128)}, u32[]{:S(2)}) copy-start(f32[25,128]{1,0:T(8,128)} %get-tuple-element.12) | copy-start | bytes 38404
  44.8 49.6 %copy-start.33 = (f32[25,128]{1,0:T(8,128)S(1)}, f32[25,128]{1,0:T(8,128)}, u32[]{:S(2)}) copy-start(f32[25,128]{1,0:T(8,128)} %get-tuple-element.50) | copy-start | bytes 38404
  44.8 49.7 %copy-start.32 = (f32[25,128]{1,0:T(8,128)S(1)}, f32[25,128]{1,0:T(8,128)}, u32[]{:S(2)}) copy-start(f32[25,128]{1,0:T(8,128)} %get-tuple-element.51) | copy-start | bytes 38404
  44.8 49.7 %copy-start.31 = (f32[25,128]{1,0:T(8,128)S(1)}, f32[25,128]{1,0:T(8,128)}, u32[]{:S(2)}) copy-start(f32[25,128]{1,0:T(8,128)} %get-tuple-element.52) | copy-start | bytes 38404
  44.8 49.7 %copy-start.29 = (f32[25,128]{1,0:T(8,128)S(1)}, f32[25,128]{1,0:T(8,128)}, u32[]{:S(2)}) copy-start(f32[25,128]{1,0:T(8,128)} %get-tuple-element.53) | copy-start | bytes 38404
  44.9 49.7 %copy-start.28 = (f32[25,128]{1,0:T(8,128)S(1)}, f32[25,128]{1,0:T(8,128)}, u32[]{:S(2)}) copy-start(f32[25,128]{1,0:T(8,128)} %get-tuple-element.54) | copy-start | bytes 38404
  44.9 49.7 %copy-start.27 = (f32[25,128]{1,0:T(8,128)S(1)}, f32[25,128]{1,0:T(8,128)}, u32[]{:S(2)}) copy-start(f32[25,128]{1,0:T(8,128)} %get-tuple-element.55) | copy-start | bytes 38404
  44.9 49.7 %copy-start.26 = (f32[25,128]{1,0:T(8,128)S(1)}, f32[25,128]{1,0:T(8,128)}, u32[]{:S(2)}) copy-start(f32[25,128]{1,0:T(8,128)} %get-tuple-element.56) | copy-start | bytes 38404
  44.9 49.7 %copy-start.25 = (f32[25,128]{1,0:T(8,128)S(1)}, f32[25,128]{1,0:T(8,128)}, u32[]{:S(2)}) copy-start(f32[25,128]{1,0:T(8,128)} %get-tuple-element.57) | copy-start | bytes 38404
  44.9 49.7 %copy-start.24 = (f32[25,128]{1,0:T(8,128)S(1)}, f32[25,128]{1,0:T(8,128)}, u32[]{:S(2)}) copy-start(f32[25,128]{1,0:T(8,128)} %get-tuple-element.58) | copy-start | bytes 38404
  44.9 49.8 %copy-start.23 = (f32[25,128]{1,0:T(8,128)S(1)}, f32[25,128]{1,0:T(8,128)}, u32[]{:S(2)}) copy-start(f32[25,128]{1,0:T(8,128)} %get-tuple-element.59) | copy-start | bytes 38404
  44.9 49.8 %copy-start.22 = (f32[25,128]{1,0:T(8,128)S(1)}, f32[25,128]{1,0:T(8,128)}, u32[]{:S(2)}) copy-start(f32[25,128]{1,0:T(8,128)} %get-tuple-element.60) | copy-start | bytes 38404
  44.9 49.8 %copy-start.21 = (f32[25,128]{1,0:T(8,128)S(1)}, f32[25,128]{1,0:T(8,128)}, u32[]{:S(2)}) copy-start(f32[25,128]{1,0:T(8,128)} %get-tuple-element.61) | copy-start | bytes 38404
  44.9 49.8 %copy-start.20 = (f32[25,128]{1,0:T(8,128)S(1)}, f32[25,128]{1,0:T(8,128)}, u32[]{:S(2)}) copy-start(f32[25,128]{1,0:T(8,128)} %get-tuple-element.62) | copy-start | bytes 38404
  46.2 45.5 %copy-start.41 = (f32[25,128]{1,0:T(8,128)S(1)}, f32[25,128]{1,0:T(8,128)}, u32[]{:S(2)}) copy-start(f32[25,128]{1,0:T(8,128)} %get-tuple-element.42) | copy-start | bytes 38404
  46.2 46.7 %copy-start.40 = (f32[25,128]{1,0:T(8,128)S(1)}, f32[25,128]{1,0:T(8,128)}, u32[]{:S(2)}) copy-start(f32[25,128]{1,0:T(8,128)} %get-tuple-element.41) | copy-start | bytes 38404
  46.2 48.0 %copy-start.39 = (f32[25,128]{1,0:T(8,128)S(1)}, f32[25,128]{1,0:T(8,128)}, u32[]{:S(2)}) copy-start(f32[25,128]{1,0:T(8,128)} %get-tuple-element.40) | copy-start | bytes 38404
  46.2 48.0 %copy-start.38 = (f32[25,128]{1,0:T(8,128)S(1)}, f32[25,128]{1,0:T(8,128)}, u32[]{:S(2)}) copy-start(f32[25,128]{1,0:T(8,128)} %get-tuple-element.39) | copy-start | bytes 38404
  46.2 48.0 %copy-start.37 = (f32[25,128]{1,0:T(8,128)S(1)}, f32[25,128]{1,0:T(8,128)}, u32[]{:S(2)}) copy-start(f32[25,128]{1,0:T(8,128)} %get-tuple-element.38) | copy-start | bytes 38404
  46.8 48.1 %copy-start.1 = (f32[5,4096]{0,1:T(8,128)S(1)}, f32[5,4096]{0,1:T(8,128)}, u32[]{:S(2)}) copy-start(f32[5,4096]{0,1:T(8,128)} %copy-done) | copy-start | bytes 245764
  47.5 61.5 %copy-start.8 = (s32[4096]{0:T(1024)}, s32[4096]{0:T(1024)S(1)}, u32[]{:S(2)}) copy-start(s32[4096]{0:T(1024)S(1)} %broadcast_clamp_fusion.1) | copy-start | bytes 49156
  134.5 387.3 %copy-start.10 = (s32[4096]{0:T(1024)}, s32[4096]{0:T(1024)S(1)}, u32[]{:S(2)}) copy-start(s32[4096]{0:T(1024)S(1)} %broadcast_clamp_fusion) | copy-start | bytes 49156
  555.0 2.4 copy-start.17
  591.5 3.8 copy-start.12
  595.3 24.9 %copy-start.15 = (f32[4096]{0:T(1024)S(1)}, f32[4096]{0:T(1024)}, u32[]{:S(2)}) copy-start(f32[4096]{0:T(1024)} %param.16) | copy-start | bytes 49156
  608.9 12.1 copy-start.45
  612.1 8.9 collective-permute-start.2
  618.1 6.6 collective-permute-start.3
  620.4 4.3 copy-start.48
  624.2 5.0 copy-start.9
  627.8 1.3 copy-start.2
  629.2 425.6 %copy-start.11 = (s32[4096]{0:T(1024)S(1)}, s32[4096]{0:T(1024)}, u32[]{:S(2)}) copy-start(s32[4096]{0:T(1024)} %copy-done.10) | copy-start | bytes 49156
  1150.2 2.4 copy-start.18
  1186.7 3.8 copy-start.13
  1190.6 23.5 %copy-start.16 = (f32[4096]{0:T(1024)S(1)}, f32[4096]{0:T(1024)}, u32[]{:S(2)}) copy-start(f32[4096]{0:T(1024)} %param.16) | copy-start | bytes 49156
  1204.1 13.6 %copy-start.4 = (f32[4096,5]{0,1:T(8,128)}, f32[4096,5]{0,1:T(8,128)S(1)}, u32[]{:S(2)}) copy-start(f32[4096,5]{0,1:T(8,128)S(1)} %copy.531) | copy-start | bytes 245764
  1204.1 10.7 copy-start.46
  1206.1 8.7 collective-permute-start.4
  1212.1 6.3 collective-permute-start.5
  1214.1 4.2 copy-start.49
Sparse Core Ops, SparseCore 0:
  26.8 432.6 all-gather.2
  629.3 425.4 all-gather.4
where the time goes:
time: 1240 us; the launch traced here: 1230 us
  waiting for transfers between devices  739 us (60%)
  local copies, waits for them, and re-layouts  311 us (25%)
  other arithmetic  95.7 us (8%)
  starting transfers between devices  33.8 us (3%)
  blocking collectives  31.8 us (3%)
  between operations  17.7 us (1%)
    all_gather x2, waiting for transfers between devices, shards(): whole = lax.all_gather(drive_vals, 'dom', axis=1, tiled=True)  738 us
    gather x4, local copies, waits for them, and re-layouts, shards(): whole[:, global_idx]  126 us
    reduce_sum x188, other arithmetic, apply_block(): return jnp.sum(matrix.reshape(nvar, nvar, -1) * vector[None, :, :], axis=1)  63.9 us
    another operation x94, local copies, waits for them, and re-layouts, apply_block(): return jnp.sum(matrix.reshape(nvar, nvar, -1) * vector[None, :, :], axis=1)  43.4 us
    gather x4, local copies, waits for them, and re-layouts, shards(): outgoing = solved[:, ret_slot]  32.6 us
    all_to_all x2, blocking collectives, shards(): lax.all_to_all(outgoing, 'dom', split_axis=1, concat_axis=1, tiled=True)  31.8 us
    gather x4, local copies, waits for them, and re-layouts, shards(): drive_vals[:, own_idx]  29.3 us
    gather x4, local copies, waits for them, and re-layouts, shards(): state_now = pooled[:, cell_src]  27.2 us
  transfers between devices with their start and end apart: 9, of which 5 were waited for; matrix products, arithmetic and copies ran while one was open for 10% of the time, Pallas kernels for 0%

commit v1 on v0

--- a/solution.py
+++ b/solution.py
@@ -87,7 +87,9 @@
     state_now = flow_state
     for sweep_idx in range(SWEEPS):
         drive_vals = drive_term(state_now)
-        whole = lax.all_gather(drive_vals, "dom", axis=1, tiled=True)
+        whole = jnp.concatenate(
+            lax.all_to_all(jnp.stack([drive_vals] * lax.axis_size("dom")), "dom", 0, 0), axis=1
+        )
         line_vals = jnp.where(remote[None, :], whole[:, global_idx], drive_vals[:, own_idx])
         solved = solve_lines(line_vals, pivot_inv, lower_blocks, upper_blocks)
         outgoing = solved[:, ret_slot]

time: 1240 us -> 641 us (0.52)
  waiting for transfers between devices: 739 us -> 80.5 us
  local copies, waits for them, and re-layouts: 311 us -> 377 us
  starting transfers between devices: 33.8 us -> 51.3 us
  between operations: 17.7 us -> 4.22 us
    all_gather x2 -> x0, waiting for transfers between devices: 738 us -> none  [shards(): whole = lax.all_gather(drive_vals, 'dom', axis=1, tiled=True)]
    all_to_all x0 -> x2, waiting for transfers between devices: none -> 76.9 us  [shards(): lax.all_to_all(jnp.stack([drive_vals] * lax.axis_size('dom')), 'dom', 0, 0)]
    reshape x0 -> x2, local copies, waits for them, and re-layouts: none -> 61.1 us  [shards(): jnp.concatenate(lax.all_to_all(jnp.stack([drive_vals] * lax.axis_size('do...]
    all_to_all x0 -> x2, starting transfers between devices: none -> 14.8 us  [shards(): lax.all_to_all(jnp.stack([drive_vals] * lax.axis_size('dom')), 'dom', 0, 0)]
  transfers between devices with their start and end apart: 9 -> 9, of which waited for: 5 -> 5; matrix products, arithmetic and copies ran while one was open for 10% -> 20% of each run, Pallas kernels for 0% -> 0%
where the time goes in v1:
time: 641 us; the launch traced here: 633 us
  local copies, waits for them, and re-layouts  377 us (59%)
  other arithmetic  84.7 us (13%)
  waiting for transfers between devices  80.5 us (13%)
  starting transfers between devices  51.3 us (8%)
  blocking collectives  34.8 us (5%)
    gather x4, local copies, waits for them, and re-layouts, shards(): whole[:, global_idx]  126 us
    all_to_all x2, waiting for transfers between devices, shards(): lax.all_to_all(jnp.stack([drive_vals] * lax.axis_size('dom')), 'dom', 0, 0)  76.9 us
    reshape x2, local copies, waits for them, and re-layouts, shards(): jnp.concatenate(lax.all_to_all(jnp.stack([drive_vals] * lax.axis_size('do...  61.1 us
    reduce_sum x188, other arithmetic, apply_block(): return jnp.sum(matrix.reshape(nvar, nvar, -1) * vector[None, :, :], axis=1)  55.3 us
    another operation x94, local copies, waits for them, and re-layouts, apply_block(): return jnp.sum(matrix.reshape(nvar, nvar, -1) * vector[None, :, :], axis=1)  44.3 us
    all_to_all x2, blocking collectives, shards(): lax.all_to_all(outgoing, 'dom', split_axis=1, concat_axis=1, tiled=True)  34.8 us
    gather x4, local copies, waits for them, and re-layouts, shards(): outgoing = solved[:, ret_slot]  32.6 us
    gather x4, local copies, waits for them, and re-layouts, shards(): drive_vals[:, own_idx]  32.6 us
  transfers between devices with their start and end apart: 9, of which 5 were waited for; matrix products, arithmetic and copies ran while one was open for 20% of the time, Pallas kernels for 0%

profile of v1, /device:TPU:1, one launch (start us, length us, event | category | flops | bytes accessed | tf_op | source)
XLA Modules:
  0.0 632.7 jit_solution(10102585403178020536)
XLA Ops:
  0.7 12.2 %all-to-all-start.1 = ((s32[32,1,128]{2,1,0:T(1,128)}), s32[32,1,128]{2,1,0:T(1,128)S(1)}, u32[]{:S(2)}, u32[]{:S(2)}) async-start(s32[32,1,128]{2,1,0:T(1,128)} %bitcast.481), calls=%async_computation.1 | async-start | bytes 32768 | tf_op jit(solution)/shard_map/all_to_all | solution.py:82
  14.2 1.5 copy.522
  16.5 2.9 collective-permute-start.1
  20.1 3.0 collective-permute-start
  24.0 1.0 collective-permute-done
  25.1 2.8 scatter_custom_fusion
  27.9 2.8 scatter_custom_fusion.1
  31.3 2.4 stack.12
  33.7 9.9 %all-to-all-start = ((f32[32,5,4096]{2,1,0:T(8,128)}), f32[32,5,4096]{2,1,0:T(8,128)}, u32[]{:S(2)}, u32[]{:S(2)}) async-start(f32[32,5,4096]{2,1,0:T(8,128)} %stack.12), calls=%async_computation | async-start | bytes 8388608 | tf_op jit(solution)/shard_map/all_to_all | solution.py:91
  49.0 2.3 slice_reduce_fusion.5
  51.5 1.0 slice_reduce_fusion.4
  53.2 1.3 reshape_squeeze.408
  54.5 1.3 reshape_squeeze.405
  55.8 1.3 reshape_squeeze.402
  57.7 1.3 reshape_squeeze.396
  63.3 1.2 slice_reduce_fusion.1
  69.5 1.3 reshape_squeeze.444
  70.9 1.3 reshape_squeeze.441
  72.2 1.3 reshape_squeeze.438
  73.5 1.3 reshape_squeeze.435
  74.8 1.3 reshape_squeeze.432
  90.7 2.9 slice_reduce_fusion.2
  96.8 1.4 fusion.25
  98.2 14.1 %gather_fusion.4 = f32[4096,5]{1,0:T(8,128)} fusion(f32[5,4096]{0,1:T(8,128)S(1)} %scatter_custom_fusion.1, s32[4096]{0:T(1024)S(1)} %broadcast_clamp_fusion.1), kind=kCustom, calls=%fused_computation.4 | custom fusion | bytes 180224 | tf_op jit(solution)/shard_map/gather | solution.py:93
  112.2 2.2 copy.528
  114.4 23.0 %gather_fusion.2 = s32[4096]{0:T(1024)S(1)} fusion(s32[4096]{0:T(1024)S(1)} %bitcast.452, s32[4096]{0:T(1024)S(1)} %broadcast_clamp_fusion.2), kind=kCustom, calls=%fused_computation.2 | custom fusion | bytes 49152 | tf_op jit(solution)/shard_map/gather | solution.py:85
  137.7 30.5 %copy.526 = f32[5,32,4096]{0,2,1:T(8,128)} copy(f32[5,32,4096]{2,0,1:T(8,128)} %bitcast.10) | data formatting | bytes 5242880 | tf_op jit(solution)/shard_map/reshape | solution.py:90
  168.3 62.3 %gather_fusion.3 = f32[4096,5]{1,0:T(8,128)S(1)} fusion(f32[5,131072]{0,1:T(8,128)} %bitcast.11, s32[4096]{0:T(1024)S(1)} %broadcast_clamp_fusion), kind=kCustom, calls=%fused_computation.3 | custom fusion | bytes 180224 | tf_op jit(solution)/shard_map/gather | solution.py:93
  231.3 0.8 multiply_reduce_fusion.187
  234.3 0.7 multiply_reduce_fusion.183
  237.5 0.7 multiply_reduce_fusion.175
  261.3 14.1 %gather_fusion.5 = f32[4096,5]{1,0:T(8,128)} fusion(f32[5,4096]{0,1:T(8,128)S(1)} %bitcast.455, s32[4096]{0:T(1024)S(1)} %copy-done.37), kind=kCustom, calls=%fused_computation.5 | custom fusion | bytes 180224 | tf_op jit(solution)/shard_map/gather | solution.py:95
  275.4 2.2 copy.530
  277.6 20.0 %all_to_all.29 = f32[5,32,128]{2,0,1:T(8,128)S(1)} all-to-all(f32[5,32,128]{2,0,1:T(8,128)S(1)} %bitcast.472), channel_id=1, replica_groups=mesh['group'=8,'dom'=32] {'dom'}, dimensions={1} | all-to-all | bytes 163840 | tf_op jit(solution)/shard_map/all_to_all | solution.py:96
  297.6 2.0 copy.531
  299.6 3.8 pad_maximum_fusion
  303.4 13.0 %gather_fusion.6 = f32[4096,5]{1,0:T(8,128)S(1)} fusion(f32[5,8192]{0,1:T(8,128)} %pad_maximum_fusion, s32[4096]{0:T(1024)S(1)} %copy-done.32), kind=kCustom, calls=%fused_computation.6 | custom fusion | bytes 180224 | tf_op jit(solution)/shard_map/gather | solution.py:98
  316.4 1.3 gather_fusion.7
  317.7 1.3 gather_fusion.8
  319.8 2.1 collective-permute-start.3
  321.9 6.3 collective-permute-start.2
  329.0 1.5 collective-permute-done.2
  330.5 3.1 scatter_custom_fusion.2
  333.6 3.2 scatter_custom_fusion.3
  337.4 2.4 stack.15
  339.8 4.9 all-to-all-start.3
  344.7 14.1 %gather_fusion.10 = f32[4096,5]{1,0:T(8,128)} fusion(f32[5,4096]{0,1:T(8,128)S(1)} %scatter_custom_fusion.3, s32[4096]{0:T(1024)S(1)} %broadcast_clamp_fusion.1), kind=kCustom, calls=%fused_computation.10 | custom fusion | bytes 180224 | tf_op jit(solution)/shard_map/gather | solution.py:93
  358.8 2.2 copy.539
  361.0 76.9 %all-to-all-done.3 = f32[32,5,4096]{2,1,0:T(8,128)} async-done(((f32[32,5,4096]{2,1,0:T(8,128)}), f32[32,5,4096]{2,1,0:T(8,128)}, u32[]{:S(2)}, u32[]{:S(2)}) %all-to-all-start.3) | async-done | bytes 2621472 | tf_op jit(solution)/shard_map/all_to_all | solution.py:91
  437.9 30.6 %copy.537 = f32[5,32,4096]{0,2,1:T(8,128)} copy(f32[5,32,4096]{2,0,1:T(8,128)} %bitcast.99) | data formatting | bytes 5242880 | tf_op jit(solution)/shard_map/reshape | solution.py:90
  468.4 62.3 %gather_fusion.9 = f32[4096,5]{1,0:T(8,128)S(1)} fusion(f32[5,131072]{0,1:T(8,128)} %bitcast.100, s32[4096]{0:T(1024)S(1)} %copy-done.31), kind=kCustom, calls=%fused_computation.9 | custom fusion | bytes 180224 | tf_op jit(solution)/shard_map/gather | solution.py:93
  531.4 0.8 multiply_reduce_fusion.93
  561.4 14.1 %gather_fusion.11 = f32[4096,5]{1,0:T(8,128)} fusion(f32[5,4096]{0,1:T(8,128)S(1)} %bitcast.453, s32[4096]{0:T(1024)S(1)} %copy-done.38), kind=kCustom, calls=%fused_computation.11 | custom fusion | bytes 180224 | tf_op jit(solution)/shard_map/gather | solution.py:95
  575.4 2.2 copy.541
  577.6 14.8 %all_to_all.30 = f32[5,32,128]{2,0,1:T(8,128)S(1)} all-to-all(f32[5,32,128]{2,0,1:T(8,128)S(1)} %bitcast.473), channel_id=1, replica_groups=mesh['group'=8,'dom'=32] {'dom'}, dimensions={1} | all-to-all | bytes 163840 | tf_op jit(solution)/shard_map/all_to_all | solution.py:96
  592.5 2.0 copy.542
  594.4 3.8 pad_maximum_fusion.1
  598.2 13.0 %gather_fusion.12 = f32[4096,5]{1,0:T(8,128)S(1)} fusion(f32[5,8192]{0,1:T(8,128)} %pad_maximum_fusion.1, s32[4096]{0:T(1024)S(1)} %copy-done.33), kind=kCustom, calls=%fused_computation.12 | custom fusion | bytes 180224 | tf_op jit(solution)/shard_map/gather | solution.py:98
  613.3 2.3 collective-permute-start.5
  615.6 7.8 %collective-permute-start.4 = (f32[5,256]{0,1:T(8,128)S(1)}, f32[5,256]{0,1:T(8,128)S(1)}, u32[]{:S(2)}, u32[]{:S(2)}) collective-permute-start(f32[5,256]{0,1:T(8,128)S(1)} %bitcast.499), channel_id=1, source_target_pairs={{0,32},{32,64},{64,96},{96,128},{128,160},{160,192},{192,224},{1,3... | collective-permute-start | bytes 15368 | tf_op jit(solution)/shard_map/ppermute | solution.py:12
  624.2 1.1 collective-permute-done.4
  625.3 3.2 scatter_custom_fusion.4
  628.5 2.9 scatter_custom_fusion.5
  631.5 1.3 copy.547
  (590 shorter events, 98.7 us)
Async XLA Ops:
  0.6 22.5 %copy-start = (f32[5,4096]{1,0:T(8,128)S(1)}, f32[5,4096]{1,0:T(8,128)}, u32[]{:S(2)}) copy-start(f32[5,4096]{1,0:T(8,128)} %param.14) | copy-start | bytes 245764
  0.6 22.6 %copy-start.34 = (f32[4096]{0:T(1024)S(1)}, f32[4096]{0:T(1024)}, u32[]{:S(2)}) copy-start(f32[4096]{0:T(1024)} %param.16) | copy-start | bytes 49156
  0.7 22.6 %copy-start.2 = (f32[5,4096]{1,0:T(8,128)S(1)}, f32[5,4096]{1,0:T(8,128)}, u32[]{:S(2)}) copy-start(f32[5,4096]{1,0:T(8,128)} %param.15) | copy-start | bytes 245764
  0.7 30.6 %all-to-all-start.1 = ((s32[32,1,128]{2,1,0:T(1,128)}), s32[32,1,128]{2,1,0:T(1,128)S(1)}, u32[]{:S(2)}, u32[]{:S(2)}) async-start(s32[32,1,128]{2,1,0:T(1,128)} %bitcast.481), calls=%async_computation.1 | async-start | bytes 32768 | tf_op jit(solution)/shard_map/all_to_all | solution.py:82
  13.5 14.3 %copy-start.44 = (s32[256,1]{0,1:T(1,128)}, s32[256,1]{0,1:T(1,128)S(1)}, u32[]{:S(2)}) copy-start(s32[256,1]{0,1:T(1,128)S(1)} %compare_select_fusion.8) | copy-start | bytes 3076
  14.2 10.8 %copy-start.45 = (s32[256,1]{0,1:T(1,128)}, s32[256,1]{0,1:T(1,128)S(1)}, u32[]{:S(2)}) copy-start(s32[256,1]{0,1:T(1,128)S(1)} %compare_select_fusion.9) | copy-start | bytes 3076
  15.8 9.3 %copy-start.40 = (f32[1,1,256]{2,1,0:T(1,128)S(1)}, f32[1,1,256]{2,1,0:T(1,128)}, u32[]{:S(2)}) copy-start(f32[1,1,256]{2,1,0:T(1,128)} %param.23) | copy-start | bytes 3076
  16.5 11.3 %collective-permute-start.1 = (f32[5,256]{0,1:T(8,128)S(1)}, f32[5,256]{0,1:T(8,128)S(1)}, u32[]{:S(2)}, u32[]{:S(2)}) collective-permute-start(f32[5,256]{0,1:T(8,128)S(1)} %bitcast.497), channel_id=1, source_target_pairs={{32,0},{64,32},{96,64},{128,96},{160,128},{192,160},{224,192},{33,... | collective-permute-start | bytes 15368 | tf_op jit(solution)/shard_map/ppermute | solution.py:12
  20.1 4.9 collective-permute-start
  23.4 4.5 copy-start.41
  33.7 10.0 %copy-start.4 = (f32[32,25,128]{2,0,1:T(8,128)S(1)}, f32[32,25,128]{2,0,1:T(8,128)}, u32[]{:S(2)}) copy-start(f32[32,25,128]{2,0,1:T(8,128)} %param.18) | copy-start | bytes 1228804
  33.7 17.7 %copy-start.3 = (f32[32,25,128]{2,0,1:T(8,128)S(1)}, f32[32,25,128]{2,0,1:T(8,128)}, u32[]{:S(2)}) copy-start(f32[32,25,128]{2,0,1:T(8,128)} %param.17) | copy-start | bytes 1228804
  33.7 104.0 %all-to-all-start = ((f32[32,5,4096]{2,1,0:T(8,128)}), f32[32,5,4096]{2,1,0:T(8,128)}, u32[]{:S(2)}, u32[]{:S(2)}) async-start(f32[32,5,4096]{2,1,0:T(8,128)} %stack.12), calls=%async_computation | async-start | bytes 8388608 | tf_op jit(solution)/shard_map/all_to_all | solution.py:91
  57.7 39.0 %copy-start.39 = (s32[32,128]{1,0:T(8,128)S(1)}, s32[32,128]{1,0:T(8,128)}, u32[]{:S(2)}) copy-start(s32[32,128]{1,0:T(8,128)} %param.25) | copy-start | bytes 49156
  137.6 30.6 %copy-start.30 = (s32[4096]{0:T(1024)}, s32[4096]{0:T(1024)S(1)}, u32[]{:S(2)}) copy-start(s32[4096]{0:T(1024)S(1)} %broadcast_clamp_fusion) | copy-start | bytes 49156
  168.2 66.9 %copy-start.13 = (f32[5,5,128]{2,1,0:T(8,128)S(1)}, f32[5,5,128]{2,1,0:T(8,128)}, u32[]{:S(2)}) copy-start(f32[5,5,128]{2,1,0:T(8,128)} %reshape_squeeze.385) | copy-start | bytes 38404
  168.2 67.7 %copy-start.11 = (f32[5,5,128]{2,1,0:T(8,128)S(1)}, f32[5,5,128]{2,1,0:T(8,128)}, u32[]{:S(2)}) copy-start(f32[5,5,128]{2,1,0:T(8,128)} %reshape_squeeze.388) | copy-start | bytes 38404
  168.2 68.4 %copy-start.9 = (f32[5,5,128]{2,1,0:T(8,128)S(1)}, f32[5,5,128]{2,1,0:T(8,128)}, u32[]{:S(2)}) copy-start(f32[5,5,128]{2,1,0:T(8,128)} %reshape_squeeze.391) | copy-start | bytes 38404
  168.2 69.2 %copy-start.7 = (f32[5,5,128]{2,1,0:T(8,128)S(1)}, f32[5,5,128]{2,1,0:T(8,128)}, u32[]{:S(2)}) copy-start(f32[5,5,128]{2,1,0:T(8,128)} %reshape_squeeze.394) | copy-start | bytes 38404
  168.2 70.0 %copy-start.6 = (f32[5,5,128]{2,1,0:T(8,128)S(1)}, f32[5,5,128]{2,1,0:T(8,128)}, u32[]{:S(2)}) copy-start(f32[5,5,128]{2,1,0:T(8,128)} %reshape_squeeze.397) | copy-start | bytes 38404
  168.3 70.8 %copy-start.5 = (f32[5,5,128]{2,1,0:T(8,128)S(1)}, f32[5,5,128]{2,1,0:T(8,128)}, u32[]{:S(2)}) copy-start(f32[5,5,128]{2,1,0:T(8,128)} %reshape_squeeze.400) | copy-start | bytes 38404
  230.6 25.9 %copy-start.12 = (f32[5,5,128]{2,1,0:T(8,128)S(1)}, f32[5,5,128]{2,1,0:T(8,128)}, u32[]{:S(2)}) copy-start(f32[5,5,128]{2,1,0:T(8,128)} %reshape_squeeze.438) | copy-start | bytes 38404
  230.6 26.7 %copy-start.10 = (f32[5,5,128]{2,1,0:T(8,128)S(1)}, f32[5,5,128]{2,1,0:T(8,128)}, u32[]{:S(2)}) copy-start(f32[5,5,128]{2,1,0:T(8,128)} %reshape_squeeze.441) | copy-start | bytes 38404
  230.6 27.4 %copy-start.8 = (f32[5,5,128]{2,1,0:T(8,128)S(1)}, f32[5,5,128]{2,1,0:T(8,128)}, u32[]{:S(2)}) copy-start(f32[5,5,128]{2,1,0:T(8,128)} %reshape_squeeze.444) | copy-start | bytes 38404
  231.2 27.6 %copy-start.28 = (f32[5,5,128]{2,1,0:T(8,128)S(1)}, f32[5,5,128]{2,1,0:T(8,128)}, u32[]{:S(2)}) copy-start(f32[5,5,128]{2,1,0:T(8,128)} %reshape_squeeze.451) | copy-start | bytes 38404
  231.2 27.7 %copy-start.22 = (f32[5,5,128]{2,1,0:T(8,128)S(1)}, f32[5,5,128]{2,1,0:T(8,128)}, u32[]{:S(2)}) copy-start(f32[5,5,128]{2,1,0:T(8,128)} %reshape_squeeze.454) | copy-start | bytes 38404
  231.2 27.8 %copy-start.14 = (f32[5,5,128]{2,1,0:T(8,128)S(1)}, f32[5,5,128]{2,1,0:T(8,128)}, u32[]{:S(2)}) copy-start(f32[5,5,128]{2,1,0:T(8,128)} %reshape_squeeze.457) | copy-start | bytes 38404
  231.2 28.0 %copy-start.26 = (f32[5,5,128]{2,1,0:T(8,128)S(1)}, f32[5,5,128]{2,1,0:T(8,128)}, u32[]{:S(2)}) copy-start(f32[5,5,128]{2,1,0:T(8,128)} %reshape_squeeze.467) | copy-start | bytes 38404
  231.2 28.1 %copy-start.24 = (f32[5,5,128]{2,1,0:T(8,128)S(1)}, f32[5,5,128]{2,1,0:T(8,128)}, u32[]{:S(2)}) copy-start(f32[5,5,128]{2,1,0:T(8,128)} %reshape_squeeze.461) | copy-start | bytes 38404
  231.2 28.1 %copy-start.20 = (f32[5,5,128]{2,1,0:T(8,128)S(1)}, f32[5,5,128]{2,1,0:T(8,128)}, u32[]{:S(2)}) copy-start(f32[5,5,128]{2,1,0:T(8,128)} %reshape_squeeze.458) | copy-start | bytes 38404
  231.2 28.2 %copy-start.18 = (f32[5,5,128]{2,1,0:T(8,128)S(1)}, f32[5,5,128]{2,1,0:T(8,128)}, u32[]{:S(2)}) copy-start(f32[5,5,128]{2,1,0:T(8,128)} %reshape_squeeze.455) | copy-start | bytes 38404
  231.3 28.2 %copy-start.16 = (f32[5,5,128]{2,1,0:T(8,128)S(1)}, f32[5,5,128]{2,1,0:T(8,128)}, u32[]{:S(2)}) copy-start(f32[5,5,128]{2,1,0:T(8,128)} %reshape_squeeze.452) | copy-start | bytes 38404
  258.9 2.5 copy-start.37
  299.6 3.8 copy-start.32
  303.4 24.8 %copy-start.35 = (f32[4096]{0:T(1024)S(1)}, f32[4096]{0:T(1024)}, u32[]{:S(2)}) copy-start(f32[4096]{0:T(1024)} %param.16) | copy-start | bytes 49156
  319.8 13.8 %collective-permute-start.3 = (f32[5,256]{0,1:T(8,128)}, f32[5,256]{0,1:T(8,128)}, u32[]{:S(2)}, u32[]{:S(2)}) collective-permute-start(f32[5,256]{0,1:T(8,128)} %bitcast.498), channel_id=1, source_target_pairs={{32,0},{64,32},{96,64},{128,96},{160,128},{192,160},{224,192},{33,... | collective-permute-start | bytes 15368 | tf_op jit(solution)/shard_map/ppermute | solution.py:12
  321.9 8.5 %collective-permute-start.2 = (f32[5,256]{0,1:T(8,128)}, f32[5,256]{0,1:T(8,128)}, u32[]{:S(2)}, u32[]{:S(2)}) collective-permute-start(f32[5,256]{0,1:T(8,128)} %bitcast.500), channel_id=1, source_target_pairs={{0,32},{32,64},{64,96},{96,128},{128,160},{160,192},{192,224},{1,3... | collective-permute-start | bytes 15368 | tf_op jit(solution)/shard_map/ppermute | solution.py:12
  328.3 5.3 copy-start.42
  339.8 98.0 %all-to-all-start.3 = ((f32[32,5,4096]{2,1,0:T(8,128)}), f32[32,5,4096]{2,1,0:T(8,128)}, u32[]{:S(2)}, u32[]{:S(2)}) async-start(f32[32,5,4096]{2,1,0:T(8,128)} %stack.15), calls=%async_computation.3 | async-start | bytes 8388608 | tf_op jit(solution)/shard_map/all_to_all | solution.py:91
  437.9 30.6 %copy-start.31 = (s32[4096]{0:T(1024)S(1)}, s32[4096]{0:T(1024)}, u32[]{:S(2)}) copy-start(s32[4096]{0:T(1024)} %copy-done.30) | copy-start | bytes 49156
  531.3 27.5 %copy-start.29 = (f32[5,5,128]{2,1,0:T(8,128)S(1)}, f32[5,5,128]{2,1,0:T(8,128)}, u32[]{:S(2)}) copy-start(f32[5,5,128]{2,1,0:T(8,128)} %reshape_squeeze.451) | copy-start | bytes 38404
  531.3 27.6 %copy-start.23 = (f32[5,5,128]{2,1,0:T(8,128)S(1)}, f32[5,5,128]{2,1,0:T(8,128)}, u32[]{:S(2)}) copy-start(f32[5,5,128]{2,1,0:T(8,128)} %reshape_squeeze.454) | copy-start | bytes 38404
  531.3 27.7 %copy-start.15 = (f32[5,5,128]{2,1,0:T(8,128)S(1)}, f32[5,5,128]{2,1,0:T(8,128)}, u32[]{:S(2)}) copy-start(f32[5,5,128]{2,1,0:T(8,128)} %reshape_squeeze.457) | copy-start | bytes 38404
  531.3 27.9 %copy-start.27 = (f32[5,5,128]{2,1,0:T(8,128)S(1)}, f32[5,5,128]{2,1,0:T(8,128)}, u32[]{:S(2)}) copy-start(f32[5,5,128]{2,1,0:T(8,128)} %reshape_squeeze.467) | copy-start | bytes 38404
  531.3 28.0 %copy-start.25 = (f32[5,5,128]{2,1,0:T(8,128)S(1)}, f32[5,5,128]{2,1,0:T(8,128)}, u32[]{:S(2)}) copy-start(f32[5,5,128]{2,1,0:T(8,128)} %reshape_squeeze.461) | copy-start | bytes 38404
  531.3 28.0 %copy-start.21 = (f32[5,5,128]{2,1,0:T(8,128)S(1)}, f32[5,5,128]{2,1,0:T(8,128)}, u32[]{:S(2)}) copy-start(f32[5,5,128]{2,1,0:T(8,128)} %reshape_squeeze.458) | copy-start | bytes 38404
  531.4 28.1 %copy-start.19 = (f32[5,5,128]{2,1,0:T(8,128)S(1)}, f32[5,5,128]{2,1,0:T(8,128)}, u32[]{:S(2)}) copy-start(f32[5,5,128]{2,1,0:T(8,128)} %reshape_squeeze.455) | copy-start | bytes 38404
  531.4 28.1 %copy-start.17 = (f32[5,5,128]{2,1,0:T(8,128)S(1)}, f32[5,5,128]{2,1,0:T(8,128)}, u32[]{:S(2)}) copy-start(f32[5,5,128]{2,1,0:T(8,128)} %reshape_squeeze.452) | copy-start | bytes 38404
  558.9 2.5 copy-start.38
  594.4 3.8 copy-start.33
  598.2 25.2 %copy-start.36 = (f32[4096]{0:T(1024)S(1)}, f32[4096]{0:T(1024)}, u32[]{:S(2)}) copy-start(f32[4096]{0:T(1024)} %param.16) | copy-start | bytes 49156
  613.3 15.2 %copy-start.1 = (f32[4096,5]{0,1:T(8,128)}, f32[4096,5]{0,1:T(8,128)S(1)}, u32[]{:S(2)}) copy-start(f32[4096,5]{0,1:T(8,128)S(1)} %copy.543) | copy-start | bytes 245764
  613.3 15.2 %collective-permute-start.5 = (f32[5,256]{0,1:T(8,128)S(1)}, f32[5,256]{0,1:T(8,128)S(1)}, u32[]{:S(2)}, u32[]{:S(2)}) collective-permute-start(f32[5,256]{0,1:T(8,128)S(1)} %bitcast.496), channel_id=1, source_target_pairs={{32,0},{64,32},{96,64},{128,96},{160,128},{192,160},{224,192},{33,... | collective-permute-start | bytes 15368 | tf_op jit(solution)/shard_map/ppermute | solution.py:12
  615.6 9.7 %collective-permute-start.4 = (f32[5,256]{0,1:T(8,128)S(1)}, f32[5,256]{0,1:T(8,128)S(1)}, u32[]{:S(2)}, u32[]{:S(2)}) collective-permute-start(f32[5,256]{0,1:T(8,128)S(1)} %bitcast.499), channel_id=1, source_target_pairs={{0,32},{32,64},{64,96},{96,128},{128,160},{160,192},{192,224},{1,3... | collective-permute-start | bytes 15368 | tf_op jit(solution)/shard_map/ppermute | solution.py:12
  623.6 4.9 copy-start.43
